TPU v7x, 32 devices: a whole 2x2x4 slice. The times are simulated.
32 devices in a mesh: grp: 2 (over x), date: 8 (over z, y), pix: 2 (over core).
Axes of the slice: x: 2, y: 2, z: 4, core: 2. Of those that a mesh axis runs over, the one named last changes fastest.
Arguments:
- slc: bfloat16 [2, 160, 16, 256], P(None, ('grp', 'date'), None, 'pix'), parts along dimension 1, may hold values from -3 to 3
- pairs: int32 [224, 2], P('grp'), parts along dimension 0, may hold values from 0 to 79, as said below
Outputs:
- phases: float32 [2, 160, 16, 256], P(None, ('grp', 'date'), None, 'pix'), parts along dimension 1
There are 2 independent parts, one for each index of `grp`. A program takes and returns all parts, laid end to end along the dimension named above; each array names one. Nothing has to cross between parts.
Inputs may be any that keep to these rules, and one draw needn't show every extreme that they name: `pairs`: each row is (i, j) with i < j <= i + 10; rows are distinct; at most 28 rows have i in one aligned block of 10 dates, and some block has exactly 28; some row has j = i + 10.
All inputs are finite; a program needn't handle non-finite values.
Results may differ from a plain program's by a relative error of at most 0.0003.
Values may be sent and summed in bfloat16 or wider, within the bound.
No kernel may reach another device: no remote copies, remote signals or barrier semaphores. Data moves between devices by JAX's collectives and lax.ppermute only.
A program may use at most 64 MiB of HBM per device.

v0:
```python
import jax
import jax.numpy as jnp
from jax import lax
from jax.sharding import PartitionSpec as P

WIN = 2
ITERS = 3


def extended(array, sides, width):
    for axis, dim in sides:
        size, length = (lax.axis_size(axis), array.shape[dim])
        up = [(i, (i + 1) % size) for i in range(size - 1)]
        down = [(j, i) for i, j in up]
        last = lax.slice_in_dim(array, length - width, length, axis=dim)
        leading = lax.slice_in_dim(array, 0, width, axis=dim)
        before = lax.ppermute(last, axis, up)
        after = lax.ppermute(leading, axis, down)
        array = jnp.concatenate([before, array, after], axis=dim)
    return array


def box_sum(values, margin):
    height = values.shape[-2] - 2 * margin
    breadth = values.shape[-1] - 2 * margin
    row_sums = values[..., 0:height, :]
    for offset in range(1, 2 * margin + 1):
        row_sums = row_sums + values[..., offset : offset + height, :]
    result = row_sums[..., 0:breadth]
    for offset in range(1, 2 * margin + 1):
        result = result + row_sums[..., offset : offset + breadth]
    return result


def coherence(first_tiles, second_tiles):
    first_re = first_tiles[0].astype(jnp.float32)
    first_im = first_tiles[1].astype(jnp.float32)
    second_re = second_tiles[0].astype(jnp.float32)
    second_im = second_tiles[1].astype(jnp.float32)
    cross_re = first_re * second_re + first_im * second_im
    cross_im = first_im * second_re - first_re * second_im
    power = (
        first_re * first_re + first_im * first_im + second_re * second_re + second_im * second_im
    )
    denom = box_sum(power, WIN)
    return (2.0 * box_sum(cross_re, WIN) / denom, 2.0 * box_sum(cross_im, WIN) / denom)


def normalize(summed):
    modulus = jnp.sqrt(summed[0] * summed[0] + summed[1] * summed[1])
    return summed / jnp.maximum(modulus, 1.0)[None]


def pair_terms(coh_re, coh_im, at_near, at_far):
    fwd_re = coh_re * at_far[0] - coh_im * at_far[1]
    fwd_im = coh_re * at_far[1] + coh_im * at_far[0]
    bwd_re = coh_re * at_near[0] + coh_im * at_near[1]
    bwd_im = coh_re * at_near[1] - coh_im * at_near[0]
    return (fwd_re, fwd_im, bwd_re, bwd_im)


def on_device(slc, pairs):
    first_dates = pairs[:, 0]
    second_dates = pairs[:, 1]
    spread_tiles = lax.all_to_all(slc, "date", split_axis=2, concat_axis=1, tiled=True)
    rim_tiles = extended(spread_tiles, (("date", 2), ("pix", 3)), WIN)
    coh_re, coh_im = coherence(
        jnp.take(rim_tiles, first_dates, axis=1), jnp.take(rim_tiles, second_dates, axis=1)
    )
    pair_count = pairs.shape[0]
    coh_re = coh_re.reshape(pair_count, -1)
    coh_im = coh_im.reshape(pair_count, -1)
    dates_all = spread_tiles.shape[1]
    pixel_count = coh_re.shape[1]
    phases = jnp.stack(
        [
            jnp.ones((dates_all, pixel_count), jnp.float32),
            jnp.zeros((dates_all, pixel_count), jnp.float32),
        ]
    )
    for iteration in range(ITERS):
        at_far = jnp.take(phases, second_dates, axis=1)
        at_near = jnp.take(phases, first_dates, axis=1)
        fwd_re, fwd_im, bwd_re, bwd_im = pair_terms(coh_re, coh_im, at_near, at_far)
        summed_re = (
            phases[0]
            + jax.ops.segment_sum(fwd_re, first_dates, num_segments=dates_all)
            + jax.ops.segment_sum(bwd_re, second_dates, num_segments=dates_all)
        )
        summed_im = (
            phases[1]
            + jax.ops.segment_sum(fwd_im, first_dates, num_segments=dates_all)
            + jax.ops.segment_sum(bwd_im, second_dates, num_segments=dates_all)
        )
        phases = normalize(jnp.stack([summed_re, summed_im]))
    banded = phases.reshape(2, dates_all, spread_tiles.shape[2], spread_tiles.shape[3])
    return lax.all_to_all(banded, "date", split_axis=1, concat_axis=2, tiled=True)


def solution(mesh):
    in_specs = (P(None, ("grp", "date"), None, "pix"), P("grp", None))
    out_specs = P(None, ("grp", "date"), None, "pix")
    return jax.shard_map(
        on_device, mesh=mesh, in_specs=in_specs, out_specs=out_specs, check_vma=False
    )
```

profile of v0, /device:TPU:0, one launch (start us, length us, event | category | flops | bytes accessed | tf_op | source)
XLA Modules:
  0.0 72.4 jit_solution(15607619028954316713)
XLA Ops:
  0.0 1.6 %copy.126 = bf16[2,10,16,128]{3,1,0,2:T(8,128)(2,1)} copy(bf16[2,10,16,128]{3,2,1,0:T(8,128)(2,1)} %param.8) | data formatting | bytes 163840 | tf_op args[0]
  1.6 7.4 %all-to-all-start = ((bf16[2,10,16,128]{3,1,0,2:T(8,128)(2,1)}), bf16[2,10,16,128]{3,1,0,2:T(8,128)(2,1)S(1)}, u32[]{:S(2)}, u32[]{:S(2)}) async-start(bf16[2,10,16,128]{3,1,0,2:T(8,128)(2,1)} %copy.126), calls=%async_computation | async-start | bytes 262144 | tf_op jit(solution)/shard_map/all_to_all | solution.py:65
  9.1 0.8 %gather_fusion.3 = f32[112,2,256]{2,1,0:T(2,128)S(1)} fusion(f32[2,80,256]{2,0,1:T(2,128)S(1)} %copy-done, s32[1024]{0:T(1024)S(1)} %pad_clamp_fusion.1), kind=kCustom, calls=%fused_computation.4.clone | custom fusion | bytes 459200 | tf_op jit(solution)/shard_map/jit(_take)/gather | solution.py:83
  9.9 0.8 %gather_fusion.2 = f32[112,2,256]{2,1,0:T(2,128)S(1)} fusion(f32[2,80,256]{2,0,1:T(2,128)S(1)} %copy-done, s32[1024]{0:T(1024)S(1)} %pad_clamp_fusion), kind=kCustom, calls=%fused_computation.1.clone | custom fusion | bytes 459200 | tf_op jit(solution)/shard_map/jit(_take)/gather | solution.py:82
  11.0 5.3 %all-to-all-done = bf16[2,10,16,128]{3,1,0,2:T(8,128)(2,1)S(1)} async-done(((bf16[2,10,16,128]{3,1,0,2:T(8,128)(2,1)}), bf16[2,10,16,128]{3,1,0,2:T(8,128)(2,1)S(1)}, u32[]{:S(2)}, u32[]{:S(2)}) %all-to-all-start) | async-done | bytes 81952 | tf_op jit(solution)/shard_map/all_to_all | solution.py:65
  16.4 2.1 %collective-permute-start = (bf16[2,80,2,128]{3,0,2,1:T(2,128)(2,1)S(1)}, bf16[2,80,2,128]{3,0,2,1:T(2,128)(2,1)S(1)}, u32[]{:S(2)}, u32[]{:S(2)}) collective-permute-start(bf16[2,80,2,128]{3,0,2,1:T(2,128)(2,1)S(1)} %bitcast.165), channel_id=1, source_target_pairs={{0,2},{2,4},{4,6},{6,8},{8,10},{10,12},{12,14},{1,3},{3,5},{5,7},{... | collective-permute-start | bytes 245768 | tf_op jit(solution)/shard_map/ppermute | solution.py:17
  18.6 1.3 %collective-permute-start.1 = (bf16[2,80,2,128]{3,0,2,1:T(2,128)(2,1)S(1)}, bf16[2,80,2,128]{3,0,2,1:T(2,128)(2,1)S(1)}, u32[]{:S(2)}, u32[]{:S(2)}) collective-permute-start(bf16[2,80,2,128]{3,0,2,1:T(2,128)(2,1)S(1)} %bitcast.166), channel_id=1, source_target_pairs={{2,0},{4,2},{6,4},{8,6},{10,8},{12,10},{14,12},{3,1},{5,3},{7,5},{... | collective-permute-start | bytes 245768 | tf_op jit(solution)/shard_map/ppermute | solution.py:18
  20.6 4.3 %collective-permute-done.1 = bf16[2,80,2,128]{3,0,2,1:T(2,128)(2,1)S(1)} collective-permute-done((bf16[2,80,2,128]{3,0,2,1:T(2,128)(2,1)S(1)}, bf16[2,80,2,128]{3,0,2,1:T(2,128)(2,1)S(1)}, u32[]{:S(2)}, u32[]{:S(2)}) %collective-permute-start.1) | collective-permute-done | bytes 81952 | tf_op jit(solution)/shard_map/ppermute | solution.py:18
  25.7 1.3 %collective-permute-start.2 = (bf16[2,80,6,2]{3,0,2,1:T(2,128)(2,1)S(1)}, bf16[2,80,6,2]{3,0,2,1:T(2,128)(2,1)S(1)}, u32[]{:S(2)}, u32[]{:S(2)}) collective-permute-start(bf16[2,80,6,2]{3,0,2,1:T(2,128)(2,1)S(1)} %get-tuple-element.20), channel_id=1, source_target_pairs={{0,1},{2,3},{4,5},{6,7},{8,9},{10,11},{12,13},{14,15},{16,17},{18,... | collective-permute-start | bytes 11528 | tf_op jit(solution)/shard_map/ppermute | solution.py:17
  27.0 1.3 %collective-permute-start.3 = (bf16[2,80,6,2]{3,0,2,1:T(2,128)(2,1)S(1)}, bf16[2,80,6,2]{3,0,2,1:T(2,128)(2,1)S(1)}, u32[]{:S(2)}, u32[]{:S(2)}) collective-permute-start(bf16[2,80,6,2]{3,0,2,1:T(2,128)(2,1)S(1)} %get-tuple-element.21), channel_id=1, source_target_pairs={{1,0},{3,2},{5,4},{7,6},{9,8},{11,10},{13,12},{15,14},{17,16},{19,... | collective-permute-start | bytes 11528 | tf_op jit(solution)/shard_map/ppermute | solution.py:18
  28.3 2.1 %collective-permute-done.3 = bf16[2,80,6,2]{3,0,2,1:T(2,128)(2,1)S(1)} collective-permute-done((bf16[2,80,6,2]{3,0,2,1:T(2,128)(2,1)S(1)}, bf16[2,80,6,2]{3,0,2,1:T(2,128)(2,1)S(1)}, u32[]{:S(2)}, u32[]{:S(2)}) %collective-permute-start.3) | collective-permute-done | bytes 3872 | tf_op jit(solution)/shard_map/ppermute | solution.py:18
  30.4 1.3 %pad_maximum_fusion = bf16[2,80,6,132]{3,0,2,1:T(2,128)(2,1)S(1)} fusion(bf16[2,80,6,2]{3,0,2,1:T(2,128)(2,1)S(1)} %collective-permute-done.3, bf16[2,80,2,128]{3,0,2,1:T(2,128)(2,1)S(1)} %collective-permute-done.1, bf16[2,80,2,128]{3,0,2,1:T(2,128)(2,1)S(1)} %bitcast.168, bf16[2,80,2,128]{3,0,2,1:T(2,128)(2,1)S(1)} %collective-permute-done, ...), kind=kLoop, calls=%fused_computation.22 | loop fusion | flops 1267200 | bytes 506880 | tf_op jit(solution)/shard_map/concatenate | solution.py:19
  31.7 2.0 %gather_fusion = bf16[112,2,6,132]{3,1,2,0:T(2,128)(2,1)S(1)} fusion(bf16[2,80,6,132]{3,0,2,1:T(2,128)(2,1)S(1)} %pad_maximum_fusion, s32[1024]{0:T(1024)S(1)} %pad_clamp_fusion.1), kind=kCustom, calls=%fused_computation.clone | custom fusion | bytes 710080 | tf_op jit(solution)/shard_map/jit(_take)/gather | solution.py:68
  33.7 2.0 %gather_fusion.1 = bf16[112,2,6,132]{3,1,2,0:T(2,128)(2,1)S(1)} fusion(bf16[2,80,6,132]{3,0,2,1:T(2,128)(2,1)S(1)} %pad_maximum_fusion, s32[1024]{0:T(1024)S(1)} %pad_clamp_fusion), kind=kCustom, calls=%fused_computation.3.clone | custom fusion | bytes 710080 | tf_op jit(solution)/shard_map/jit(_take)/gather | solution.py:68
  37.9 2.0 %multiply_add_fusion.1 = (f32[1,112,6,132]{1,0,3,2:T(1,128)S(1)}, f32[1,112,6,132]{1,0,3,2:T(1,128)S(1)}, f32[1,112,6,132]{1,0,3,2:T(1,128)S(1)}) fusion(bf16[2,112,6,132]{1,0,3,2:T(2,128)(2,1)S(1)} %get-tuple-element.38, bf16[2,112,6,132]{1,0,3,2:T(2,128)(2,1)S(1)} %get-tuple-element.39), kind=kLoop, calls=%fused_computation.34 | loop fusion | flops 1507968 | bytes 1774080 | tf_op jit(solution)/shard_map/add | solution.py:40
  40.6 1.2 %scatter_custom_fusion.1 = f32[80,256]{1,0:T(8,128)S(1)} fusion(s32[112]{0:T(128)S(1)} %get-tuple-element.34, f32[112,256]{1,0:T(8,128)S(1)} %copy.151, f32[112,256]{1,0:T(8,128)S(1)} %copy.150, f32[2,112,256]{2,1,0:T(8,128)S(1)} %fusion.6, f32[]{:T(128)} %constant.36.clone.1), kind=kCustom, calls=%fused_computation.133 | custom fusion | flops 114688 | bytes 540676 | tf_op jit(solution)/shard_map/scatter-add | solution.py:88
  41.8 1.2 %scatter_custom_fusion.3 = f32[80,256]{1,0:T(8,128)S(1)} fusion(s32[112]{0:T(128)S(1)} %get-tuple-element.34, f32[112,256]{1,0:T(8,128)S(1)} %copy.151, f32[112,256]{1,0:T(8,128)S(1)} %copy.150, f32[2,112,256]{2,1,0:T(8,128)S(1)} %fusion.6, f32[]{:T(128)} %constant.36.clone.1), kind=kCustom, calls=%fused_computation.128 | custom fusion | flops 114688 | bytes 540676 | tf_op jit(solution)/shard_map/scatter-add | solution.py:93
  43.0 1.4 %scatter_custom_fusion.2 = f32[80,256]{1,0:T(8,128)S(1)} fusion(s32[112]{0:T(128)S(1)} %get-tuple-element.35, f32[112,256]{1,0:T(8,128)S(1)} %copy.150, f32[112,256]{1,0:T(8,128)S(1)} %copy.151, f32[1,112,256]{2,0,1:T(1,128)S(1)} %get-tuple-element.23, f32[1,112,256]{2,0,1:T(1,128)S(1)} %get-tuple-element.22, f32[]{:T(128)} %constant.36.clone.1), kind=kCustom, calls=%fused_computation.95 | custom fusion | flops 114688 | bytes 540676 | tf_op jit(solution)/shard_map/scatter-add | solution.py:92
  44.4 1.2 %scatter_custom_fusion = f32[80,256]{1,0:T(8,128)S(1)} fusion(s32[112]{0:T(128)S(1)} %get-tuple-element.35, f32[112,256]{1,0:T(8,128)S(1)} %copy.151, f32[112,256]{1,0:T(8,128)S(1)} %copy.150, f32[1,112,256]{2,0,1:T(1,128)S(1)} %get-tuple-element.23, f32[1,112,256]{2,0,1:T(1,128)S(1)} %get-tuple-element.22, f32[]{:T(128)} %constant.33.clone.1), kind=kCustom, calls=%fused_computation.93 | custom fusion | flops 114688 | bytes 540676 | tf_op jit(solution)/shard_map/scatter-add | solution.py:87
  45.9 0.8 %gather_fusion.5 = f32[112,2,256]{2,1,0:T(2,128)S(1)} fusion(f32[2,80,256]{2,0,1:T(2,128)S(1)} %copy_divide_fusion, s32[1024]{0:T(1024)S(1)} %pad_clamp_fusion.1), kind=kCustom, calls=%fused_computation.5.clone | custom fusion | bytes 459200 | tf_op jit(solution)/shard_map/jit(_take)/gather | solution.py:83
  46.7 0.8 %gather_fusion.4 = f32[112,2,256]{2,1,0:T(2,128)S(1)} fusion(f32[2,80,256]{2,0,1:T(2,128)S(1)} %copy_divide_fusion, s32[1024]{0:T(1024)S(1)} %pad_clamp_fusion), kind=kCustom, calls=%fused_computation.2.clone | custom fusion | bytes 459200 | tf_op jit(solution)/shard_map/jit(_take)/gather | solution.py:82
  47.8 1.2 %scatter_custom_fusion.5 = f32[80,256]{1,0:T(8,128)S(1)} fusion(s32[112]{0:T(128)S(1)} %get-tuple-element.34, f32[112,256]{1,0:T(8,128)S(1)} %copy.151, f32[112,256]{1,0:T(8,128)S(1)} %copy.150, f32[2,112,256]{2,1,0:T(8,128)S(1)} %fusion.4, f32[]{:T(128)} %constant.36.clone.1), kind=kCustom, calls=%fused_computation.120 | custom fusion | flops 114688 | bytes 540676 | tf_op jit(solution)/shard_map/scatter-add | solution.py:88
  49.0 1.2 %scatter_custom_fusion.7 = f32[80,256]{1,0:T(8,128)S(1)} fusion(s32[112]{0:T(128)S(1)} %get-tuple-element.34, f32[112,256]{1,0:T(8,128)S(1)} %copy.151, f32[112,256]{1,0:T(8,128)S(1)} %copy.150, f32[2,112,256]{2,1,0:T(8,128)S(1)} %fusion.4, f32[]{:T(128)} %constant.36.clone.1), kind=kCustom, calls=%fused_computation.112 | custom fusion | flops 114688 | bytes 540676 | tf_op jit(solution)/shard_map/scatter-add | solution.py:93
  50.3 1.2 %scatter_custom_fusion.4 = f32[80,256]{1,0:T(8,128)S(1)} fusion(f32[80,256]{1,0:T(8,128)S(1)} %bitcast.173, s32[112]{0:T(128)S(1)} %get-tuple-element.35, f32[112,256]{1,0:T(8,128)S(1)} %copy.151, f32[112,256]{1,0:T(8,128)S(1)} %copy.150, f32[2,112,256]{2,1,0:T(8,128)S(1)} %fusion.5), kind=kCustom, calls=%fused_computation.124 | custom fusion | flops 114688 | bytes 540672 | tf_op jit(solution)/shard_map/scatter-add | solution.py:87
  51.6 1.2 %scatter_custom_fusion.6 = f32[80,256]{1,0:T(8,128)S(1)} fusion(f32[80,256]{1,0:T(8,128)S(1)} %bitcast.174, s32[112]{0:T(128)S(1)} %get-tuple-element.35, f32[112,256]{1,0:T(8,128)S(1)} %copy.151, f32[112,256]{1,0:T(8,128)S(1)} %copy.150, f32[2,112,256]{2,1,0:T(8,128)S(1)} %fusion.5), kind=kCustom, calls=%fused_computation.116 | custom fusion | flops 114688 | bytes 540672 | tf_op jit(solution)/shard_map/scatter-add | solution.py:92
  53.1 0.8 %gather_fusion.7 = f32[112,2,256]{2,1,0:T(2,128)S(1)} fusion(f32[2,80,256]{2,0,1:T(2,128)S(1)} %copy.141, s32[1024]{0:T(1024)S(1)} %pad_clamp_fusion.1), kind=kCustom, calls=%fused_computation.7.clone | custom fusion | bytes 459200 | tf_op jit(solution)/shard_map/jit(_take)/gather | solution.py:83
  53.9 0.8 %gather_fusion.6 = f32[112,2,256]{2,1,0:T(2,128)S(1)} fusion(f32[2,80,256]{2,0,1:T(2,128)S(1)} %copy.141, s32[1024]{0:T(1024)S(1)} %pad_clamp_fusion), kind=kCustom, calls=%fused_computation.6.clone | custom fusion | bytes 459200 | tf_op jit(solution)/shard_map/jit(_take)/gather | solution.py:82
  54.8 1.2 %scatter_custom_fusion.11 = f32[80,256]{1,0:T(8,128)S(1)} fusion(s32[112]{0:T(128)S(1)} %get-tuple-element.34, f32[112,256]{1,0:T(8,128)S(1)} %copy.151, f32[112,256]{1,0:T(8,128)S(1)} %copy.150, f32[2,112,256]{2,1,0:T(8,128)S(1)} %fusion.2, f32[]{:T(128)} %constant.36.clone.1), kind=kCustom, calls=%fused_computation.96 | custom fusion | flops 114688 | bytes 540676 | tf_op jit(solution)/shard_map/scatter-add | solution.py:93
  56.1 1.2 %scatter_custom_fusion.9 = f32[80,256]{1,0:T(8,128)S(1)} fusion(s32[112]{0:T(128)S(1)} %get-tuple-element.34, f32[112,256]{1,0:T(8,128)S(1)} %copy.151, f32[112,256]{1,0:T(8,128)S(1)} %copy.150, f32[2,112,256]{2,1,0:T(8,128)S(1)} %fusion.2, f32[]{:T(128)} %constant.36.clone.1), kind=kCustom, calls=%fused_computation.104 | custom fusion | flops 114688 | bytes 540676 | tf_op jit(solution)/shard_map/scatter-add | solution.py:88
  57.4 1.2 %scatter_custom_fusion.10 = f32[80,256]{1,0:T(8,128)S(1)} fusion(f32[80,256]{1,0:T(8,128)S(1)} %get-tuple-element.24, s32[112]{0:T(128)S(1)} %get-tuple-element.35, f32[112,256]{1,0:T(8,128)S(1)} %copy.151, f32[112,256]{1,0:T(8,128)S(1)} %copy.150, f32[2,112,256]{2,1,0:T(8,128)S(1)} %fusion.3), kind=kCustom, calls=%fused_computation.100 | custom fusion | flops 114688 | bytes 540672 | tf_op jit(solution)/shard_map/scatter-add | solution.py:92
  58.6 1.2 %scatter_custom_fusion.8 = f32[80,256]{1,0:T(8,128)S(1)} fusion(f32[80,256]{1,0:T(8,128)S(1)} %get-tuple-element.25, s32[112]{0:T(128)S(1)} %get-tuple-element.35, f32[112,256]{1,0:T(8,128)S(1)} %copy.151, f32[112,256]{1,0:T(8,128)S(1)} %copy.150, f32[2,112,256]{2,1,0:T(8,128)S(1)} %fusion.3), kind=kCustom, calls=%fused_computation.108 | custom fusion | flops 114688 | bytes 540672 | tf_op jit(solution)/shard_map/scatter-add | solution.py:87
  60.2 11.6 %all_to_all.36 = f32[2,80,2,128]{3,2,0,1:T(2,128)S(1)} all-to-all(f32[2,80,2,128]{3,2,0,1:T(2,128)S(1)} %maximum_divide_fusion.1), channel_id=1, replica_groups=mesh['grp'=2,'date'=8,'pix'=2] {'date'}, dimensions={1} | all-to-all | bytes 327680 | tf_op jit(solution)/shard_map/all_to_all | solution.py:97
  (49 shorter events, 6.6 us)
Async XLA Ops:
  1.6 7.4 %copy-start.1 = (s32[112,2]{0,1:T(2,128)S(1)}, s32[112,2]{0,1:T(2,128)}, u32[]{:S(2)}) copy-start(s32[112,2]{0,1:T(2,128)} %param.9) | copy-start | bytes 2692
  1.6 7.5 %copy-start = (f32[2,80,256]{2,0,1:T(2,128)S(1)}, f32[2,80,256]{2,0,1:T(2,128)}, u32[]{:S(2)}) copy-start(f32[2,80,256]{2,0,1:T(2,128)} %constant.19.clone.2) | copy-start | bytes 491524
  1.6 14.8 %all-to-all-start = ((bf16[2,10,16,128]{3,1,0,2:T(8,128)(2,1)}), bf16[2,10,16,128]{3,1,0,2:T(8,128)(2,1)S(1)}, u32[]{:S(2)}, u32[]{:S(2)}) async-start(bf16[2,10,16,128]{3,1,0,2:T(8,128)(2,1)} %copy.126), calls=%async_computation | async-start | bytes 262144 | tf_op jit(solution)/shard_map/all_to_all | solution.py:65
  16.4 4.2 %collective-permute-start = (bf16[2,80,2,128]{3,0,2,1:T(2,128)(2,1)S(1)}, bf16[2,80,2,128]{3,0,2,1:T(2,128)(2,1)S(1)}, u32[]{:S(2)}, u32[]{:S(2)}) collective-permute-start(bf16[2,80,2,128]{3,0,2,1:T(2,128)(2,1)S(1)} %bitcast.165), channel_id=1, source_target_pairs={{0,2},{2,4},{4,6},{6,8},{8,10},{10,12},{12,14},{1,3},{3,5},{5,7},{... | collective-permute-start | bytes 245768 | tf_op jit(solution)/shard_map/ppermute | solution.py:17
  18.6 6.3 %collective-permute-start.1 = (bf16[2,80,2,128]{3,0,2,1:T(2,128)(2,1)S(1)}, bf16[2,80,2,128]{3,0,2,1:T(2,128)(2,1)S(1)}, u32[]{:S(2)}, u32[]{:S(2)}) collective-permute-start(bf16[2,80,2,128]{3,0,2,1:T(2,128)(2,1)S(1)} %bitcast.166), channel_id=1, source_target_pairs={{2,0},{4,2},{6,4},{8,6},{10,8},{12,10},{14,12},{3,1},{5,3},{7,5},{... | collective-permute-start | bytes 245768 | tf_op jit(solution)/shard_map/ppermute | solution.py:18
  25.7 2.6 %collective-permute-start.2 = (bf16[2,80,6,2]{3,0,2,1:T(2,128)(2,1)S(1)}, bf16[2,80,6,2]{3,0,2,1:T(2,128)(2,1)S(1)}, u32[]{:S(2)}, u32[]{:S(2)}) collective-permute-start(bf16[2,80,6,2]{3,0,2,1:T(2,128)(2,1)S(1)} %get-tuple-element.20), channel_id=1, source_target_pairs={{0,1},{2,3},{4,5},{6,7},{8,9},{10,11},{12,13},{14,15},{16,17},{18,... | collective-permute-start | bytes 11528 | tf_op jit(solution)/shard_map/ppermute | solution.py:17
  27.0 3.4 %collective-permute-start.3 = (bf16[2,80,6,2]{3,0,2,1:T(2,128)(2,1)S(1)}, bf16[2,80,6,2]{3,0,2,1:T(2,128)(2,1)S(1)}, u32[]{:S(2)}, u32[]{:S(2)}) collective-permute-start(bf16[2,80,6,2]{3,0,2,1:T(2,128)(2,1)S(1)} %get-tuple-element.21), channel_id=1, source_target_pairs={{1,0},{3,2},{5,4},{7,6},{9,8},{11,10},{13,12},{15,14},{17,16},{19,... | collective-permute-start | bytes 11528 | tf_op jit(solution)/shard_map/ppermute | solution.py:18
where the time goes:
time: 72.8 us; the launch traced here: 72.4 us
  other arithmetic  20.5 us (28%)
  local copies, waits for them, and re-layouts  14.2 us (20%)
  starting transfers between devices  13.5 us (19%)
  waiting for transfers between devices  12.3 us (17%)
  blocking collectives  11.6 us (16%)
    all_to_all x1, blocking collectives, on_device(): lax.all_to_all(banded, 'date', split_axis=1, concat_axis=2, tiled=True)  11.6 us
    all_to_all x1, starting transfers between devices, on_device(): lax.all_to_all(slc, 'date', split_axis=2, concat_axis=1, tiled=True)  7.44 us
    ppermute x2, waiting for transfers between devices, extended(): after = lax.ppermute(leading, axis, down)  6.38 us
    all_to_all x1, waiting for transfers between devices, on_device(): lax.all_to_all(slc, 'date', split_axis=2, concat_axis=1, tiled=True)  5.32 us
    scatter-add x3, other arithmetic, on_device(): jax.ops.segment_sum(fwd_im, first_dates, num_segments=dates_all)  3.87 us
    scatter-add x3, other arithmetic, on_device(): jax.ops.segment_sum(fwd_re, first_dates, num_segments=dates_all)  3.69 us
    scatter-add x3, other arithmetic, on_device(): jax.ops.segment_sum(bwd_im, second_dates, num_segments=dates_all)  3.62 us
    scatter-add x3, other arithmetic, on_device(): jax.ops.segment_sum(bwd_re, second_dates, num_segments=dates_all)  3.62 us
  transfers between devices with their start and end apart: 5, of which 4 were waited for; matrix products, arithmetic and copies ran while one was open for 3% of the time, Pallas kernels for 0%

commit v1 on v0

v1 whole, which is shorter than its diff:
```python
import functools

import jax
import jax.numpy as jnp
from jax import lax
from jax.experimental import pallas as pl
from jax.experimental.pallas import tpu as pltpu
from jax.sharding import PartitionSpec as P

WIN = 2
ITERS = 3
GAP = 10
LANES = 128


def pack_edges(slc_ref, edge_ref):
    comps, dates, rows, cols = slc_ref.shape
    lead = (1 - lax.axis_index("pix")) * WIN
    lane = lax.broadcasted_iota(jnp.int32, (rows, cols), 1)
    acc = jnp.zeros((rows, cols), jnp.float32)
    for c in range(comps):
        for k in range(dates):
            place = WIN * (c * dates + k)
            tile = slc_ref[c, k].astype(jnp.float32)
            moved = pltpu.roll(tile, lead + place, 1)
            acc = jnp.where((lane >= place) & (lane < place + WIN), moved, acc)
    edge_ref[...] = acc.astype(edge_ref.dtype)


def link_kernel(
    pairs_ref, mine_ref, mate_ref, cross_ref, za_ref, zb_ref, out_ref,
    sre, sim, hre, him, power, are, aim, bre, bim, cre, cim, stage,
    list_i, list_j, second, third, *, unroll,
):
    _, dates, rows, cols = out_ref.shape
    tiles = 2 * dates + 1
    block = lax.axis_index("date")
    pix = lax.axis_index("pix")
    odd = block % 2
    far = (block // 2) % 2
    base = dates * (2 * (block // 2) - 3)
    own = (3 + odd) * dates
    lane = lax.broadcasted_iota(jnp.int32, (rows, cols), 1)
    outer = pix * (cols - WIN)
    facing = (lane >= outer) & (lane < outer + WIN)
    pitch = rows + 8
    stage[...] = jnp.zeros_like(stage)

    def box(center, halo, slot):
        total = center
        for shift in range(1, WIN + 1):
            left = jnp.where(lane < shift, halo, center)
            right = jnp.where(lane >= cols - shift, halo, center)
            total = total + pltpu.roll(left, cols - shift, 1)
            total = total + pltpu.roll(right, shift, 1)
        start = 8 + slot * pitch
        stage[pl.ds(start, rows), :] = total
        result = total
        for shift in range(1, WIN + 1):
            result = result + stage[pl.ds(start - shift, rows), :]
            result = result + stage[pl.ds(start + shift, rows), :]
        return result

    def load_block(ref, first, slot):
        edge = ref[first + tiles - 1].astype(jnp.float32)
        edge = pltpu.roll(edge, -WIN * pix & (cols - 1), 1)

        def one(step, carry):
            for u in range(2):
                k = step * 2 + u
                where = slot * dates + k
                re = ref[first + k].astype(jnp.float32)
                im = ref[first + dates + k].astype(jnp.float32)
                hr = jnp.where(facing, pltpu.roll(edge, -WIN * k & (cols - 1), 1), 0.0)
                hi = jnp.where(facing, pltpu.roll(edge, -WIN * (dates + k) & (cols - 1), 1), 0.0)
                sre[where] = re
                sim[where] = im
                hre[where] = hr
                him[where] = hi
                power[where] = box(re * re + im * im, hr * hr + hi * hi, u)
            return carry

        lax.fori_loop(0, dates // 2, one, 0)

    load_block(mine_ref, 0, 3 + odd)
    load_block(mate_ref, 0, 4 - odd)
    load_block(cross_ref, 0, 7 * odd)
    up, down = 5 - 4 * far, 1 + 4 * far
    load_block(za_ref, 0, up + odd)
    load_block(za_ref, tiles, up + 1 - odd)
    load_block(zb_ref, 0, down + odd)
    load_block(zb_ref, tiles, down + 1 - odd)

    def select(p, counts):
        n1, n2, n3 = counts
        i = pairs_ref[2 * p] - base
        j = pairs_ref[2 * p + 1] - base
        list_i[n1] = i
        list_j[n1] = j
        second[n2] = n1
        third[n3] = n1

        def within(reach):
            low, high = own - reach * dates, own + (reach + 1) * dates
            return ((j >= low) & (i < high)).astype(jnp.int32)

        return n1 + within(2), n2 + within(1), n3 + within(0)

    zero = jnp.int32(0)
    n1, n2, n3 = lax.fori_loop(0, pairs_ref.shape[0] // 2, select, (zero, zero, zero))

    def start(w, carry):
        are[w] = jnp.ones((rows, cols), jnp.float32)
        aim[w] = jnp.zeros((rows, cols), jnp.float32)
        return carry

    lax.fori_loop(0, are.shape[0], start, 0)

    def cohere(p, slot):
        i, j = list_i[p], list_j[p]

        def cross(fr, fi, sr, si):
            return fr * sr + fi * si, fi * sr - fr * si

        main = cross(sre[i], sim[i], sre[j], sim[j])
        rim = cross(hre[i], him[i], hre[j], him[j])
        scale = 2.0 / (power[i] + power[j])
        re = box(main[0], rim[0], 2 * slot) * scale
        im = box(main[1], rim[1], 2 * slot + 1) * scale
        cre[p] = re
        cim[p] = im
        are[i] = are[i] + re
        aim[i] = aim[i] + im
        are[j] = are[j] + re
        aim[j] = aim[j] - im

    def groups(count, width, body):
        def several(q, carry):
            for u in range(width):
                body(q * width + u, u)
            return carry

        whole = count // width
        lax.fori_loop(0, whole, several, 0)
        lax.fori_loop(whole * width, count, lambda p, carry: (body(p, 0), carry)[1], 0)

    groups(n1, unroll, cohere)

    def normal(w, xr, xi, yr, yi):
        re, im = xr[w], xi[w]
        scale = lax.rsqrt(jnp.maximum(re * re + im * im, 1.0))
        re, im = re * scale, im * scale
        xr[w] = re
        xi[w] = im
        yr[w] = re
        yi[w] = im

    def step(index, count, xr, xi, yr, yi):
        def one(q, u):
            p = index[q]
            i, j = list_i[p], list_j[p]
            re, im = cre[p], cim[p]
            nr, ni, fr, fi = xr[i], xi[i], xr[j], xi[j]
            yr[i] = yr[i] + (re * fr - im * fi)
            yi[i] = yi[i] + (re * fi + im * fr)
            yr[j] = yr[j] + (re * nr + im * ni)
            yi[j] = yi[j] + (re * ni - im * nr)

        groups(count, unroll, one)

    def settle(low, count, xr, xi, yr, yi):
        def two(q, carry):
            for u in range(2):
                normal(low + 2 * q + u, xr, xi, yr, yi)
            return carry

        lax.fori_loop(0, count // 2, two, 0)

    settle(own - 2 * dates, 5 * dates, are, aim, bre, bim)
    step(second, n2, are, aim, bre, bim)
    settle(own - dates, 3 * dates, bre, bim, are, aim)
    step(third, n3, bre, bim, are, aim)

    def finish(k, carry):
        re, im = are[own + k], aim[own + k]
        scale = lax.rsqrt(jnp.maximum(re * re + im * im, 1.0))
        out_ref[0, k] = re * scale
        out_ref[1, k] = im * scale
        return carry

    lax.fori_loop(0, dates, finish, 0)


def swap(array, axis, matching):
    return lax.ppermute(array, axis, [*matching, *((j, i) for i, j in matching)])


def on_device(slc, pairs):
    comps, dates, rows, cols = slc.shape
    size = lax.axis_size("date")
    pair_count = pairs.shape[0]
    assert lax.axis_size("pix") == 2 and size % 2 == 0 and cols == LANES
    assert GAP <= dates and dates % 2 == 0 and comps * dates * WIN <= cols and rows % 8 == 0

    vmem = pl.BlockSpec(memory_space=pltpu.VMEM)
    edge = pl.pallas_call(
        pack_edges,
        out_shape=jax.ShapeDtypeStruct((rows, cols), slc.dtype),
        in_specs=[vmem],
        out_specs=vmem,
    )(slc)
    edge = swap(edge, "pix", [(0, 1)])
    mine = jnp.concatenate([slc.reshape(comps * dates, rows, cols), edge[None]], axis=0)

    def matching(step, keep):
        return [(i, i + step) for i in range(size - step) if keep(i)]

    cross = swap(mine, "date", matching(3, lambda i: i % 2 == 1))
    mate = swap(mine, "date", matching(1, lambda i: i % 2 == 0))
    both = jnp.concatenate([mine, mate], axis=0)
    za = swap(both, "date", matching(2, lambda i: i // 2 % 2 == 0))
    zb = swap(both, "date", matching(2, lambda i: i // 2 % 2 == 1))

    window = 8 * dates
    unroll = max(1, 64 // rows)
    field = pltpu.VMEM((window, rows, cols), jnp.float32)
    pair_field = pltpu.VMEM((pair_count, rows, cols), jnp.float32)
    stage = pltpu.VMEM((8 + 2 * unroll * (rows + 8) + 8, cols), jnp.float32)
    index = pltpu.SMEM((pair_count,), jnp.int32)
    return pl.pallas_call(
        functools.partial(link_kernel, unroll=unroll),
        out_shape=jax.ShapeDtypeStruct((comps, dates, rows, cols), jnp.float32),
        in_specs=[pl.BlockSpec(memory_space=pltpu.SMEM)] + [vmem] * 5,
        out_specs=vmem,
        scratch_shapes=[field] * 9 + [pair_field] * 2 + [stage] + [index] * 4,
        compiler_params=pltpu.CompilerParams(vmem_limit_bytes=60 * 1024 * 1024),
    )(pairs.reshape(-1), mine, mate, cross, za, zb)


def solution(mesh):
    in_specs = (P(None, ("grp", "date"), None, "pix"), P("grp", None))
    out_specs = P(None, ("grp", "date"), None, "pix")
    return jax.shard_map(
        on_device, mesh=mesh, in_specs=in_specs, out_specs=out_specs, check_vma=False
    )
```

time: 72.8 us -> 39.1 us (0.54)
  the two profiles are of different devices: /device:TPU:0 before, /device:TPU:14 now
where the time goes in v1:
time: 39.1 us; the launch traced here: 38.9 us
  Pallas kernels  17.6 us (45%)
  waiting for transfers between devices  10.9 us (28%)
  starting transfers between devices  7.54 us (19%)
  local copies, waits for them, and re-layouts  2.76 us (7%)
    pallas_call x1, Pallas kernels, on_device(): pl.pallas_call(functools.partial(link_kernel, unroll=unroll), out_shape=j...  16 us
    ppermute x5, waiting for transfers between devices, swap(): lax.ppermute(array, axis, [*matching, *((j, i) for i, j in matching)])  10.9 us
    ppermute x5, starting transfers between devices, swap(): lax.ppermute(array, axis, [*matching, *((j, i) for i, j in matching)])  7.54 us
    unnamed x15, local copies, waits for them, and re-layouts  2.07 us
    pallas_call x1, Pallas kernels, on_device(): pl.pallas_call(pack_edges, out_shape=jax.ShapeDtypeStruct((rows, cols), s...  1.65 us
  transfers between devices with their start and end apart: 5, of which 3 were waited for; matrix products, arithmetic and copies ran while one was open for 2% of the time, Pallas kernels for 0%

profile of v1, /device:TPU:14, one launch (start us, length us, event | category | flops | bytes accessed | tf_op | source)
XLA Modules:
  0.0 38.9 jit_solution(14185738369298614320)
XLA Ops:
  0.0 0.0 copy-start
  0.0 1.6 %shard_map.28 = bf16[16,128]{1,0:T(8,128)(2,1)} custom-call(bf16[2,10,16,128]{3,2,1,0:T(8,128)(2,1)} %slc_ref.1), custom_call_target="tpu_custom_call" | custom-call | tf_op jit(solution)/shard_map/pallas_call | solution.py:206
  1.7 0.0 collective-permute-start
  1.7 1.4 %collective-permute-done = bf16[16,128]{1,0:T(8,128)(2,1)S(1)} collective-permute-done((bf16[16,128]{1,0:T(8,128)(2,1)}, bf16[16,128]{1,0:T(8,128)(2,1)S(1)}, u32[]{:S(2)}, u32[]{:S(2)}) %collective-permute-start) | collective-permute-done | bytes 4128 | tf_op jit(solution)/shard_map/ppermute | solution.py:195
  3.0 0.0 copy-done
  3.0 0.0 copy-start.1
  3.1 0.0 copy-start.6
  3.1 0.6 %collective-permute-start.1 = (bf16[21,16,128]{2,1,0:T(8,128)(2,1)S(1)}, bf16[21,16,128]{2,1,0:T(8,128)(2,1)S(1)}, u32[]{:S(2)}, u32[]{:S(2)}) collective-permute-start(bf16[21,16,128]{2,1,0:T(8,128)(2,1)S(1)} %pad_maximum_fusion.1.mine_ref), channel_id=1, source_target_pairs={{0,2},{4,6},{8,10},{12,14},{2,0},{6,4},{10,8},{14,12},{1,3},{5,7},... | collective-permute-start | bytes 258056 | tf_op jit(solution)/shard_map/ppermute | solution.py:195
  3.6 4.1 %collective-permute-done.1.mate_ref = bf16[21,16,128]{2,1,0:T(8,128)(2,1)S(1)} collective-permute-done((bf16[21,16,128]{2,1,0:T(8,128)(2,1)S(1)}, bf16[21,16,128]{2,1,0:T(8,128)(2,1)S(1)}, u32[]{:S(2)}, u32[]{:S(2)}) %collective-permute-start.1) | collective-permute-done | bytes 86048 | tf_op jit(solution)/shard_map/ppermute | solution.py:195
  7.7 0.0 copy-start.2
  7.8 0.6 %copy-done.2 = bf16[21,16,128]{2,1,0:T(8,128)(2,1)} copy-done((bf16[21,16,128]{2,1,0:T(8,128)(2,1)}, bf16[21,16,128]{2,1,0:T(8,128)(2,1)S(1)}, u32[]{:S(2)}) %copy-start.2) | copy-done | bytes 86040
  8.4 0.4 %collective-permute-start.3 = (bf16[42,16,128]{2,1,0:T(8,128)(2,1)S(1)}, bf16[42,16,128]{2,1,0:T(8,128)(2,1)S(1)}, u32[]{:S(2)}, u32[]{:S(2)}) collective-permute-start(bf16[42,16,128]{2,1,0:T(8,128)(2,1)S(1)} %pad_maximum_fusion), channel_id=1, source_target_pairs={{0,4},{2,6},{8,12},{10,14},{4,0},{6,2},{12,8},{14,10},{1,5},{3,7},... | collective-permute-start | bytes 516104 | tf_op jit(solution)/shard_map/ppermute | solution.py:195
  8.8 4.6 %collective-permute-start.4 = (bf16[42,16,128]{2,1,0:T(8,128)(2,1)S(1)}, bf16[42,16,128]{2,1,0:T(8,128)(2,1)S(1)}, u32[]{:S(2)}, u32[]{:S(2)}) collective-permute-start(bf16[42,16,128]{2,1,0:T(8,128)(2,1)S(1)} %pad_maximum_fusion), channel_id=1, source_target_pairs={{4,8},{6,10},{8,4},{10,6},{5,9},{7,11},{9,5},{11,7},{20,24},{22,26... | collective-permute-start | bytes 516104 | tf_op jit(solution)/shard_map/ppermute | solution.py:195
  13.4 0.0 copy-done.1
  13.4 1.9 %collective-permute-start.2 = (bf16[21,16,128]{2,1,0:T(8,128)(2,1)S(1)}, bf16[21,16,128]{2,1,0:T(8,128)(2,1)S(1)}, u32[]{:S(2)}, u32[]{:S(2)}) collective-permute-start(bf16[21,16,128]{2,1,0:T(8,128)(2,1)S(1)} %pad_maximum_fusion.1.mine_ref), channel_id=1, source_target_pairs={{2,8},{6,12},{8,2},{12,6},{3,9},{7,13},{9,3},{13,7},{18,24},{22,28... | collective-permute-start | bytes 258056 | tf_op jit(solution)/shard_map/ppermute | solution.py:195
  15.4 0.0 copy-done.6
  15.4 0.1 copy.3
  15.5 0.7 %reshape.6.pairs_ref = s32[224]{0:T(256)} reshape(s32[112,2]{1,0:T(8,128)S(1)} %copy.3) | data formatting | bytes 1792 | tf_op jit(solution)/shard_map/reshape | solution.py:237
  16.2 5.4 %collective-permute-done.2.cross_ref = bf16[21,16,128]{2,1,0:T(8,128)(2,1)S(1)} collective-permute-done((bf16[21,16,128]{2,1,0:T(8,128)(2,1)S(1)}, bf16[21,16,128]{2,1,0:T(8,128)(2,1)S(1)}, u32[]{:S(2)}, u32[]{:S(2)}) %collective-permute-start.2) | collective-permute-done | bytes 86048 | tf_op jit(solution)/shard_map/ppermute | solution.py:195
  21.6 0.0 copy-start.5
  21.6 0.0 collective-permute-done.3.za_ref
  21.6 0.0 copy-start.3
  21.6 0.0 collective-permute-done.4.zb_ref
  21.6 0.6 %copy-done.5 = bf16[21,16,128]{2,1,0:T(8,128)(2,1)} copy-done((bf16[21,16,128]{2,1,0:T(8,128)(2,1)}, bf16[21,16,128]{2,1,0:T(8,128)(2,1)S(1)}, u32[]{:S(2)}) %copy-start.5) | copy-done | bytes 86040
  22.2 0.1 copy-done.3
  22.3 0.0 copy-start.4
  22.3 0.7 %copy-done.4 = bf16[42,16,128]{2,1,0:T(8,128)(2,1)} copy-done((bf16[42,16,128]{2,1,0:T(8,128)(2,1)}, bf16[42,16,128]{2,1,0:T(8,128)(2,1)S(1)}, u32[]{:S(2)}) %copy-start.4) | copy-done | bytes 172056
  23.0 16.0 %shard_map.29 = f32[2,10,16,128]{3,2,1,0:T(8,128)} custom-call(s32[224]{0:T(256)} %reshape.6.pairs_ref, bf16[21,16,128]{2,1,0:T(8,128)(2,1)} %copy-done.1, bf16[21,16,128]{2,1,0:T(8,128)(2,1)} %copy-done.2, bf16[21,16,128]{2,1,0:T(8,128)(2,1)} %copy-done.5, bf16[42,16,128]{2,1,0:T(8,128)(2,1)} %copy-done.3, bf16[42,16,128]{2,1,0:T(8,128)(2,1)} %copy-done.4), custom_call_target="tpu_custom_call" | custom-call | tf_op jit(solution)/shard_map/pallas_call | solution.py:230
  (2 shorter events, 0.0 us)
Async XLA Ops:
  0.0 3.0 %copy-start = (bf16[2,10,16,128]{3,2,1,0:T(8,128)(2,1)S(1)}, bf16[2,10,16,128]{3,2,1,0:T(8,128)(2,1)}, u32[]{:S(2)}) copy-start(bf16[2,10,16,128]{3,2,1,0:T(8,128)(2,1)} %slc_ref.1) | copy-start | bytes 245764
  1.7 1.4 %collective-permute-start = (bf16[16,128]{1,0:T(8,128)(2,1)}, bf16[16,128]{1,0:T(8,128)(2,1)S(1)}, u32[]{:S(2)}, u32[]{:S(2)}) collective-permute-start(bf16[16,128]{1,0:T(8,128)(2,1)} %shard_map.28), channel_id=1, source_target_pairs={{0,1},{1,0},{2,3},{3,2},{4,5},{5,4},{6,7},{7,6},{8,9},{9,8},{10,11... | collective-permute-start | bytes 12296 | tf_op jit(solution)/shard_map/ppermute | solution.py:195
  3.0 10.4 %copy-start.1 = (bf16[21,16,128]{2,1,0:T(8,128)(2,1)}, bf16[21,16,128]{2,1,0:T(8,128)(2,1)S(1)}, u32[]{:S(2)}) copy-start(bf16[21,16,128]{2,1,0:T(8,128)(2,1)S(1)} %pad_maximum_fusion.1.mine_ref) | copy-start | bytes 258052
  3.1 12.3 %copy-start.6 = (s32[112,2]{0,1:T(2,128)S(1)}, s32[112,2]{0,1:T(2,128)}, u32[]{:S(2)}) copy-start(s32[112,2]{0,1:T(2,128)} %param.3) | copy-start | bytes 2692
  3.1 4.7 %collective-permute-start.1 = (bf16[21,16,128]{2,1,0:T(8,128)(2,1)S(1)}, bf16[21,16,128]{2,1,0:T(8,128)(2,1)S(1)}, u32[]{:S(2)}, u32[]{:S(2)}) collective-permute-start(bf16[21,16,128]{2,1,0:T(8,128)(2,1)S(1)} %pad_maximum_fusion.1.mine_ref), channel_id=1, source_target_pairs={{0,2},{4,6},{8,10},{12,14},{2,0},{6,4},{10,8},{14,12},{1,3},{5,7},... | collective-permute-start | bytes 258056 | tf_op jit(solution)/shard_map/ppermute | solution.py:195
  7.7 0.6 %copy-start.2 = (bf16[21,16,128]{2,1,0:T(8,128)(2,1)}, bf16[21,16,128]{2,1,0:T(8,128)(2,1)S(1)}, u32[]{:S(2)}) copy-start(bf16[21,16,128]{2,1,0:T(8,128)(2,1)S(1)} %collective-permute-done.1.mate_ref) | copy-start | bytes 258052
  8.4 13.2 %collective-permute-start.3 = (bf16[42,16,128]{2,1,0:T(8,128)(2,1)S(1)}, bf16[42,16,128]{2,1,0:T(8,128)(2,1)S(1)}, u32[]{:S(2)}, u32[]{:S(2)}) collective-permute-start(bf16[42,16,128]{2,1,0:T(8,128)(2,1)S(1)} %pad_maximum_fusion), channel_id=1, source_target_pairs={{0,4},{2,6},{8,12},{10,14},{4,0},{6,2},{12,8},{14,10},{1,5},{3,7},... | collective-permute-start | bytes 516104 | tf_op jit(solution)/shard_map/ppermute | solution.py:195
  8.8 12.8 %collective-permute-start.4 = (bf16[42,16,128]{2,1,0:T(8,128)(2,1)S(1)}, bf16[42,16,128]{2,1,0:T(8,128)(2,1)S(1)}, u32[]{:S(2)}, u32[]{:S(2)}) collective-permute-start(bf16[42,16,128]{2,1,0:T(8,128)(2,1)S(1)} %pad_maximum_fusion), channel_id=1, source_target_pairs={{4,8},{6,10},{8,4},{10,6},{5,9},{7,11},{9,5},{11,7},{20,24},{22,26... | collective-permute-start | bytes 516104 | tf_op jit(solution)/shard_map/ppermute | solution.py:195
  13.4 8.2 %collective-permute-start.2 = (bf16[21,16,128]{2,1,0:T(8,128)(2,1)S(1)}, bf16[21,16,128]{2,1,0:T(8,128)(2,1)S(1)}, u32[]{:S(2)}, u32[]{:S(2)}) collective-permute-start(bf16[21,16,128]{2,1,0:T(8,128)(2,1)S(1)} %pad_maximum_fusion.1.mine_ref), channel_id=1, source_target_pairs={{2,8},{6,12},{8,2},{12,6},{3,9},{7,13},{9,3},{13,7},{18,24},{22,28... | collective-permute-start | bytes 258056 | tf_op jit(solution)/shard_map/ppermute | solution.py:195
  21.6 0.6 %copy-start.5 = (bf16[21,16,128]{2,1,0:T(8,128)(2,1)}, bf16[21,16,128]{2,1,0:T(8,128)(2,1)S(1)}, u32[]{:S(2)}) copy-start(bf16[21,16,128]{2,1,0:T(8,128)(2,1)S(1)} %collective-permute-done.2.cross_ref) | copy-start | bytes 258052
  21.6 0.7 %copy-start.3 = (bf16[42,16,128]{2,1,0:T(8,128)(2,1)}, bf16[42,16,128]{2,1,0:T(8,128)(2,1)S(1)}, u32[]{:S(2)}) copy-start(bf16[42,16,128]{2,1,0:T(8,128)(2,1)S(1)} %collective-permute-done.3.za_ref) | copy-start | bytes 516100
  22.3 0.7 %copy-start.4 = (bf16[42,16,128]{2,1,0:T(8,128)(2,1)}, bf16[42,16,128]{2,1,0:T(8,128)(2,1)S(1)}, u32[]{:S(2)}) copy-start(bf16[42,16,128]{2,1,0:T(8,128)(2,1)S(1)} %collective-permute-done.4.zb_ref) | copy-start | bytes 516100
